TPU v7x, 32 devices: a whole 2x2x4 slice. The times are simulated.
32 devices in a mesh: dp: 2 (over y), seq: 4 (over z), tensor: 4 (over x, core).
Axes of the slice: x: 2, y: 2, z: 4, core: 2. Of those that a mesh axis runs over, the one named last changes fastest.
Arguments:
- layer_input: bfloat16 [6, 1024, 2048], P('dp', 'seq'), may hold values from -6 to 6
- lengths: int32 [6], P('dp'), may hold values from 256 to 1024, as said below
- cotangent: bfloat16 [6, 1024, 2048], P('dp', ('seq', 'tensor')), may hold values from -6 to 6
- ln1_gain: bfloat16 [2048], replicated, may hold values from 0.5 to 1.5
- ln1_bias: bfloat16 [2048], replicated, may hold values from -3 to 3
- w_query: bfloat16 [2048, 2048], P(None, 'tensor'), may hold values from -0.125 to 0.125
- b_query: bfloat16 [2048], P('tensor'), may hold values from -3 to 3
- w_kv: bfloat16 [2048, 256], replicated, may hold values from -0.125 to 0.125
- b_value: bfloat16 [128], replicated, may hold values from -3 to 3
- w_out: bfloat16 [2048, 2048], P('tensor'), may hold values from -0.5 to 0.5
- b_out: bfloat16 [2048], replicated, may hold values from -3 to 3
- ln2_gain: bfloat16 [2048], replicated, may hold values from 0.5 to 1.5
- ln2_bias: bfloat16 [2048], replicated, may hold values from -3 to 3
- w_up: bfloat16 [2048, 8192], P(None, 'tensor'), may hold values from -0.125 to 0.125
- b_up: bfloat16 [8192], P('tensor'), may hold values from -3 to 3
- w_down: bfloat16 [8192, 2048], P('tensor'), may hold values from -0.0625 to 0.0625
- b_down: bfloat16 [2048], replicated, may hold values from -3 to 3
Outputs:
- layer_output: bfloat16 [6, 1024, 2048], P('dp', ('seq', 'tensor'))
- input_grad: float32 [6, 1024, 2048], P('dp', ('seq', 'tensor'))
- g_w_query: float32 [2048, 2048], P(('dp', 'seq'), 'tensor')
- g_b_query: float32 [16, 128], P('tensor', ('dp', 'seq'))
- g_w_kv: float32 [2048, 256], P(('dp', 'seq', 'tensor'))
- g_b_value: float32 [128], P(('dp', 'seq', 'tensor'))
- g_w_out: float32 [2048, 2048], P('tensor', ('dp', 'seq'))
- g_w_up: float32 [2048, 8192], P(('dp', 'seq'), 'tensor')
- g_b_up: float32 [64, 128], P('tensor', ('dp', 'seq'))
- g_w_down: float32 [8192, 2048], P('tensor', ('dp', 'seq'))
- g_norms_biases: float32 [6, 2048], P(None, ('dp', 'seq', 'tensor'))
Inputs may be any that keep to these rules, and one draw needn't show every extreme that they name: `lengths`: the number of real tokens at the start of each row; the rest of the row is padding.
All inputs are finite; a program needn't handle non-finite values.
Results may differ from a plain program's by a relative error of at most 0.012.
Values may be sent and summed in bfloat16 or wider, within the bound.
A program may use at most 256 MiB of HBM per device.

v0:
```python
import math
import jax
import jax.numpy as jnp
from jax import lax
from jax.sharding import PartitionSpec as P

NORM_EPS = 1e-05


def normalize(values_in):
    row_mean = jnp.mean(values_in, -1, keepdims=True)
    centered = values_in - row_mean
    variance = jnp.mean(centered * centered, -1, keepdims=True)
    inv_std = lax.rsqrt(variance + NORM_EPS)
    return (centered * inv_std, inv_std)


def norm_back(grad_in, normed, inv_std, norm_gain):
    scaled = grad_in * norm_gain
    mean_scaled = jnp.mean(scaled, -1, keepdims=True)
    mean_mixed = jnp.mean(scaled * normed, -1, keepdims=True)
    return inv_std * (scaled - mean_scaled - normed * mean_mixed)


def across_rows(left_in, right_in):
    return lax.dot_general(
        left_in, right_in, (((0,), (0,)), ((), ())), preferred_element_type=jnp.float32
    )


def times_transposed(left_in, right_in):
    return lax.dot_general(
        left_in, right_in, (((1,), (1,)), ((), ())), preferred_element_type=jnp.float32
    )


def shards(
    layer_input,
    lengths,
    cotangent,
    ln1_gain,
    ln1_bias,
    w_query,
    b_query,
    w_kv,
    b_value,
    w_out,
    b_out,
    ln2_gain,
    ln2_bias,
    w_up,
    b_up,
    w_down,
    b_down,
):
    n_rows, seq_len, model_width = layer_input.shape
    share_len = seq_len // lax.axis_size("tensor")
    tensor_index = lax.axis_index("tensor")
    seq_index = lax.axis_index("seq")
    full_len = seq_len * lax.axis_size("seq")
    head_size = w_kv.shape[1] // 2
    num_heads = w_query.shape[1] // head_size
    q_scale = 1.0 / math.sqrt(head_size)

    def own_rows(values_in):
        return lax.dynamic_slice_in_dim(values_in, tensor_index * share_len, share_len, 1)

    positions = seq_index * seq_len + jnp.arange(seq_len, dtype=jnp.int32)
    key_places = jnp.arange(full_len, dtype=jnp.int32)
    is_valid = (positions[None, :] < lengths[:, None]).astype(jnp.float32)
    allowed_keys = (key_places[None, None, :] <= positions[None, :, None]) & (
        key_places[None, None, :] < lengths[:, None, None]
    )
    valid_own = own_rows(is_valid)
    x_float = layer_input.astype(jnp.float32)
    normed_x1, inv_one = normalize(x_float)
    normed_one = (normed_x1 * ln1_gain + ln1_bias).astype(jnp.bfloat16)
    flat_one = normed_one.reshape(n_rows * seq_len, model_width)
    queries = (
        (jnp.dot(flat_one, w_query, preferred_element_type=jnp.float32) + b_query) * q_scale
    ).astype(jnp.bfloat16)
    queries = queries.reshape(n_rows, seq_len, num_heads, head_size)
    kv_bias = jnp.concatenate([jnp.zeros((head_size,), jnp.float32), b_value.astype(jnp.float32)])
    kv_local = (jnp.dot(flat_one, w_kv, preferred_element_type=jnp.float32) + kv_bias).astype(
        jnp.bfloat16
    )
    kv_local = kv_local.reshape(n_rows, seq_len, 2 * head_size)
    kv_all = lax.all_gather(kv_local, "seq", axis=1, tiled=True)
    key_rows = kv_all[..., :head_size]
    value_rows = kv_all[..., head_size:]

    def scores_of(query_rows):
        raw_scores = jnp.einsum(
            "rshd,rld->rhsl", query_rows, key_rows, preferred_element_type=jnp.float32
        )
        return jnp.where(allowed_keys[:, None], raw_scores, -1e30)

    scores = scores_of(queries)
    row_max = jnp.max(scores, -1, keepdims=True)
    exp_scores = jnp.exp(scores - row_max)
    exp_total = jnp.sum(exp_scores, -1, keepdims=True)
    soft_probs = exp_scores / exp_total
    log_total = row_max + jnp.log(exp_total)
    mixed_heads = jnp.einsum(
        "rhsl,rld->rshd",
        soft_probs.astype(jnp.bfloat16),
        value_rows,
        preferred_element_type=jnp.float32,
    ).astype(jnp.bfloat16)
    mixed_heads = mixed_heads.reshape(n_rows * seq_len, num_heads * head_size)
    attn_part = jnp.dot(mixed_heads, w_out, preferred_element_type=jnp.float32).reshape(
        n_rows, seq_len, model_width
    )
    residual = x_float + (lax.psum(attn_part, "tensor") + b_out)
    normed_x2, inv_two = normalize(residual)
    normed_two = (normed_x2 * ln2_gain + ln2_bias).astype(jnp.bfloat16)
    resid_own = own_rows(residual)
    normed_x2_own = own_rows(normed_x2)
    flat_two = normed_two.reshape(n_rows * seq_len, model_width)
    pre_act = jnp.dot(flat_two, w_up, preferred_element_type=jnp.float32) + b_up
    activated, gelu_pull = jax.vjp(
        lambda inner_in: jax.nn.gelu(inner_in, approximate=True), pre_act
    )
    act_low = activated.astype(jnp.bfloat16)
    mlp_part = jnp.dot(act_low, w_down, preferred_element_type=jnp.float32).reshape(
        n_rows, seq_len, model_width
    )
    mlp_own = (
        lax.psum_scatter(
            mlp_part.astype(jnp.bfloat16), "tensor", scatter_dimension=1, tiled=True
        ).astype(jnp.float32)
        + b_down
    )
    y_own = (valid_own[..., None] * (resid_own + mlp_own)).astype(jnp.bfloat16)
    cot_full = lax.all_gather(cotangent, "tensor", axis=1, tiled=True)
    grad_y = cot_full.astype(jnp.float32) * is_valid[..., None]
    grad_y_low = grad_y.astype(jnp.bfloat16).reshape(n_rows * seq_len, model_width)
    grad_y_own = cotangent.astype(jnp.float32) * valid_own[..., None]
    g_w_down = across_rows(act_low, grad_y_low)
    grad_act = times_transposed(grad_y_low, w_down)
    grad_pre = gelu_pull(grad_act)[0].astype(jnp.bfloat16)
    g_w_up = across_rows(flat_two, grad_pre)
    g_b_up = jnp.sum(grad_pre.astype(jnp.float32), axis=0)
    grad_a2 = times_transposed(grad_pre, w_up).reshape(n_rows, seq_len, model_width)
    grad_n2 = lax.psum(grad_a2, "tensor")
    grad_resid = grad_y + norm_back(grad_n2, normed_x2, inv_two, ln2_gain)
    grad_resid_low = grad_resid.astype(jnp.bfloat16)
    grad_resid_own = own_rows(grad_resid)
    grad_n2_own = own_rows(grad_n2)
    grad_resid_own_low = own_rows(grad_resid_low)
    g_ln2_gain = jnp.sum(grad_n2_own * normed_x2_own, axis=(0, 1))
    g_ln2_bias = jnp.sum(grad_n2_own, axis=(0, 1))
    g_b_out = jnp.sum(grad_resid_own_low.astype(jnp.float32), axis=(0, 1))
    g_b_down = jnp.sum(grad_y_own, axis=(0, 1))
    flat_resid = grad_resid_low.reshape(n_rows * seq_len, model_width)
    g_w_out = across_rows(mixed_heads, flat_resid)
    grad_mixed = times_transposed(flat_resid, w_out).astype(jnp.bfloat16)
    grad_mixed = grad_mixed.reshape(n_rows, seq_len, num_heads, head_size)
    again_probs = jnp.exp(scores_of(queries) - log_total)
    grad_probs = jnp.einsum(
        "rshd,rld->rhsl", grad_mixed, value_rows, preferred_element_type=jnp.float32
    )
    inner_sum = jnp.sum(again_probs * grad_probs, -1, keepdims=True)
    grad_scores = (again_probs * (grad_probs - inner_sum)).astype(jnp.bfloat16)
    grad_query = jnp.einsum(
        "rhsl,rld->rshd", grad_scores, key_rows, preferred_element_type=jnp.float32
    ).astype(jnp.bfloat16)
    grad_keys = jnp.einsum(
        "rhsl,rshd->rld", grad_scores, queries, preferred_element_type=jnp.float32
    )
    grad_values = jnp.einsum(
        "rhsl,rshd->rld",
        again_probs.astype(jnp.bfloat16),
        grad_mixed,
        preferred_element_type=jnp.float32,
    )
    grad_kv = jnp.concatenate([grad_keys, grad_values], -1)
    grad_kv_own = lax.psum_scatter(
        grad_kv, ("seq", "tensor"), scatter_dimension=1, tiled=True
    ).astype(jnp.bfloat16)
    flat_query = grad_query.reshape(n_rows * seq_len, num_heads * head_size)
    g_w_query = across_rows(flat_one, flat_query) * q_scale
    g_b_query = jnp.sum(flat_query.astype(jnp.float32), axis=0) * q_scale
    grad_n1_part = (times_transposed(flat_query, w_query) * q_scale).reshape(
        n_rows, seq_len, model_width
    )
    grad_n1_own = lax.psum_scatter(
        grad_n1_part.astype(jnp.bfloat16), "tensor", scatter_dimension=1, tiled=True
    ).astype(jnp.float32)
    flat_kv = grad_kv_own.reshape(n_rows * share_len, 2 * head_size)
    grad_n1_own = grad_n1_own + times_transposed(flat_kv, w_kv).reshape(
        n_rows, share_len, model_width
    )
    one_own = own_rows(normed_one).reshape(n_rows * share_len, model_width)
    g_w_kv = across_rows(one_own, flat_kv)
    g_b_value = jnp.sum(flat_kv[:, head_size:].astype(jnp.float32), axis=0)
    normed_x1_own = own_rows(normed_x1)
    x_grad_own = grad_resid_own + norm_back(grad_n1_own, normed_x1_own, own_rows(inv_one), ln1_gain)
    g_ln1_gain = jnp.sum(grad_n1_own * normed_x1_own, axis=(0, 1))
    g_ln1_bias = jnp.sum(grad_n1_own, axis=(0, 1))
    query_table = g_b_query.reshape(num_heads, head_size)
    up_table = g_b_up.reshape(-1, 128)
    summed = (
        lax.psum_scatter(g_w_query, ("dp", "seq"), scatter_dimension=0, tiled=True),
        lax.psum_scatter(query_table, ("dp", "seq"), scatter_dimension=1, tiled=True),
        lax.psum_scatter(g_w_out, ("dp", "seq"), scatter_dimension=1, tiled=True),
        lax.psum_scatter(g_w_up, ("dp", "seq"), scatter_dimension=0, tiled=True),
        lax.psum_scatter(up_table, ("dp", "seq"), scatter_dimension=1, tiled=True),
        lax.psum_scatter(g_w_down, ("dp", "seq"), scatter_dimension=1, tiled=True),
    )
    small_grads = jnp.stack([g_ln1_gain, g_ln1_bias, g_ln2_gain, g_ln2_bias, g_b_out, g_b_down])
    shared = (
        lax.psum_scatter(g_w_kv, ("dp", "seq", "tensor"), scatter_dimension=0, tiled=True),
        lax.psum_scatter(small_grads, ("dp", "seq", "tensor"), scatter_dimension=1, tiled=True),
        lax.psum_scatter(g_b_value, ("dp", "seq", "tensor"), scatter_dimension=0, tiled=True),
    )
    return (
        y_own,
        x_grad_own,
        summed[0],
        summed[1],
        shared[0],
        shared[2],
        summed[2],
        summed[3],
        summed[4],
        summed[5],
        shared[1],
    )


def solution(mesh):
    placed = (
        P("dp", "seq", None),
        P("dp"),
        P("dp", ("seq", "tensor"), None),
        P(),
        P(),
        P(None, "tensor"),
        P("tensor"),
        P(),
        P(),
        P("tensor", None),
        P(),
        P(),
        P(),
        P(None, "tensor"),
        P("tensor"),
        P("tensor", None),
        P(),
    )
    return jax.shard_map(
        shards,
        mesh=mesh,
        in_specs=placed,
        out_specs=(
            P("dp", ("seq", "tensor"), None),
            P("dp", ("seq", "tensor"), None),
            P(("dp", "seq"), "tensor"),
            P("tensor", ("dp", "seq")),
            P(("dp", "seq", "tensor"), None),
            P(("dp", "seq", "tensor")),
            P("tensor", ("dp", "seq")),
            P(("dp", "seq"), "tensor"),
            P("tensor", ("dp", "seq")),
            P("tensor", ("dp", "seq")),
            P(None, ("dp", "seq", "tensor")),
        ),
        check_vma=False,
    )
```

profile of v0, /device:TPU:0, one launch (start us, length us, event | category | flops | bytes accessed | tf_op | source)
XLA Modules:
  0.0 1648.8 jit_solution(9399819819224728491)
XLA Ops:
  21.5 5.2 multiply_convert_fusion.3
  30.5 29.8 %all-gather.3.cloned.1.call-done = bf16[3,1024,256]{2,1,0:T(8,128)(2,1)} async-done(((bf16[3,256,256]{2,1,0:T(8,128)(2,1)}), bf16[3,1024,256]{2,1,0:T(8,128)(2,1)}) %all-gather.3.cloned.1.call-update) | async-done | bytes 1572880 | tf_op jit(solution)/shard_map/all_gather | solution.py:88
  60.4 7.9 fusion.4
  68.3 7.4 fusion.3
  75.8 6.5 fusion.28
  93.4 117.9 %all-reduce.7.cloned.1.call-done = f32[3,256,2048]{2,1,0:T(8,128)} async-done(((f32[3,256,2048]{2,1,0:T(8,128)}), f32[3,256,2048]{2,1,0:T(8,128)}) %all-reduce.7.cloned.1.call-update) | async-done | bytes 6291472 | tf_op jit(solution)/shard_map/psum | solution.py:114
  211.3 4.6 fusion.48
  224.9 8.5 fusion.49
  233.4 14.9 convert_reduce_fusion.1
  248.3 8.6 fusion.50
  257.0 13.3 convolution_convert_fusion
  270.3 106.6 %all-reduce.9.cloned.1.call-done = f32[3,256,2048]{2,1,0:T(8,128)} async-done(((f32[3,256,2048]{2,1,0:T(8,128)}), f32[3,256,2048]{2,1,0:T(8,128)}) %all-reduce.9.cloned.1.call-update) | async-done | bytes 6291472 | tf_op jit(solution)/shard_map/psum | solution.py:145
  376.9 5.9 multiply_reduce_fusion.2
  384.2 6.1 fusion.47
  399.3 8.6 fusion
  407.9 6.7 fusion.2
  421.6 5.3 multiply_convert_fusion
  429.4 9.6 fusion.25
  439.0 6.1 convolution_bitcast_fusion.1
  449.8 5.0 copy.69
  454.8 98.2 %all-reduce.10 = bf16[3,1024,256]{2,0,1:T(4,128)(2,1)} all-reduce(f32[3,1024,256]{2,0,1:T(4,128)} %copy.69), channel_id=4, replica_groups=mesh['dp'=2,'seq'=4,'tensor'=4] {'seq','tensor'}, use_global_device_ids=true, to_apply=%region_13.14.clone | all-reduce | flops 786432 | bytes 4718592
  570.2 6.0 fusion.32
  576.3 5.7 convolution_multiply_fusion
  582.3 13.9 fusion.45
  596.3 12.5 fusion.51
  611.0 40.6 %all-reduce.2 = f32[128]{0:T(128)S(1)} all-reduce(f32[128]{0:T(128)S(1)} %convert_reduce_fusion.4), channel_id=8, replica_groups=mesh['dp'=2,'seq'=4,'tensor'=4] {'dp','seq','tensor'}, use_global_device_ids=true, to_apply=%region_21.22.clone | all-reduce | flops 128 | bytes 1024
  657.5 99.5 %reduce-scatter.35.cloned.1.call-done = f32[64,6]{1,0:T(8,128)} async-done(((f32[2048,6]{1,0:T(8,128)}), f32[64,6]{1,0:T(8,128)}) %reduce-scatter.35.cloned.1.call-update) | async-done | bytes 1552
  758.4 135.5 %reduce-scatter.23.cloned.1.call-done = f32[64,256]{1,0:T(8,128)} async-done(((f32[2048,256]{1,0:T(8,128)}), f32[64,256]{1,0:T(8,128)}) %reduce-scatter.23.cloned.1.call-update) | async-done | bytes 65552 | tf_op jit(solution)/shard_map/reduce_scatter | solution.py:213
  893.9 89.4 %reduce-scatter.25.cloned.1.call-done = f32[512,256]{1,0:T(8,128)} async-done(((f32[512,2048]{1,0:T(8,128)}), f32[512,256]{1,0:T(8,128)}) %reduce-scatter.25.cloned.1.call-update) | async-done | bytes 524304 | tf_op jit(solution)/shard_map/reduce_scatter | solution.py:206
  983.4 92.0 %reduce-scatter.21.cloned.1.call-done = f32[256,512]{1,0:T(8,128)} async-done(((f32[2048,512]{1,0:T(8,128)}), f32[256,512]{1,0:T(8,128)}) %reduce-scatter.21.cloned.1.call-update) | async-done | bytes 524304 | tf_op jit(solution)/shard_map/reduce_scatter | solution.py:204
  1075.4 283.5 %reduce-scatter.29.cloned.1.call-done = f32[2048,256]{1,0:T(8,128)} async-done(((f32[2048,2048]{1,0:T(8,128)}), f32[2048,256]{1,0:T(8,128)}) %reduce-scatter.29.cloned.1.call-update) | async-done | bytes 2097168 | tf_op jit(solution)/shard_map/reduce_scatter | solution.py:209
  1358.9 282.9 %reduce-scatter.27.cloned.1.call-done = f32[256,2048]{1,0:T(8,128)} async-done(((f32[2048,2048]{1,0:T(8,128)}), f32[256,2048]{1,0:T(8,128)}) %reduce-scatter.27.cloned.1.call-update) | async-done | bytes 2097168 | tf_op jit(solution)/shard_map/reduce_scatter | solution.py:207
  (164 shorter events, 88.9 us)
Async XLA Ops:
  7.2 76.0 %copy-start = (bf16[512,2048]{1,0:T(8,128)(2,1)S(1)}, bf16[512,2048]{1,0:T(8,128)(2,1)}, u32[]{:S(2)}) copy-start(bf16[512,2048]{1,0:T(8,128)(2,1)} %param.26) | copy-start | bytes 6291460
  7.2 6.4 copy-start.22
  7.2 6.4 copy-start.23
  7.2 53.2 %all-gather.3.cloned.1.call-start = ((), (), s32[]{:S(2)}) async-start(), calls=%async_computation.10 | async-start | bytes 1966080 | tf_op jit(solution)/shard_map/all_gather | solution.py:88
  7.3 6.4 copy-start.3
  20.5 68.9 %all-gather.5.cloned.1.call-start = ((), (), s32[]{:S(2)}) async-start(), calls=%async_computation.13 | async-start | bytes 3932160 | tf_op jit(solution)/shard_map/all_gather | solution.py:135
  21.2 190.1 %all-reduce.7.cloned.1.call-start = ((), (), s32[]{:S(2)}) async-start(), calls=%async_computation.11 | async-start | bytes 12582912 | tf_op jit(solution)/shard_map/psum | solution.py:114
  21.5 8.2 copy-start.29
  68.3 7.5 copy-start.9
  87.7 289.2 %all-reduce.9.cloned.1.call-start = ((), (), s32[]{:S(2)}) async-start(), calls=%async_computation.14 | async-start | bytes 12582912 | tf_op jit(solution)/shard_map/psum | solution.py:145
  215.9 6.2 copy-start.1
  216.7 8.2 slice-start.1
  222.1 11.3 copy-start.14
  224.9 8.5 copy-start.13
  248.3 8.6 copy-start.32
  256.9 300.6 %reduce-scatter.17.cloned.1.call-start = ((), (), s32[]{:S(2)}) async-start(), calls=%async_computation.12 | async-start | bytes 3932160 | tf_op jit(solution)/shard_map/reduce_scatter | solution.py:129
  270.2 290.2 %reduce-scatter.19.cloned.1.call-start = ((), (), s32[]{:S(2)}) async-start(), calls=%async_computation.15 | async-start | bytes 3932160 | tf_op jit(solution)/shard_map/reduce_scatter | solution.py:187
  376.9 6.4 copy-start.4
  376.9 7.3 copy-start.6
  407.9 9.5 copy-start.10
  426.9 182.6 %reduce-scatter.33.cloned.1.call-start = ((), (), s32[]{:S(2)}) async-start(), calls=%async_computation.22 | async-start | bytes 73728
  429.1 223.1 %reduce-scatter.31.cloned.1.call-start = ((), (), s32[]{:S(2)}) async-start(), calls=%async_computation.21 | async-start | bytes 73728
  429.4 9.6 copy-start.7
  454.8 102.7 %copy-start.15 = (bf16[3,64,2048]{2,1,0:T(8,128)(2,1)S(1)}, bf16[3,64,2048]{2,1,0:T(8,128)(2,1)}, u32[]{:S(2)}) copy-start(bf16[3,64,2048]{2,1,0:T(8,128)(2,1)} %param.19) | copy-start | bytes 2359300
  454.8 105.7 %copy-start.19 = (f32[2048]{0:T(1024)S(1)}, f32[2048]{0:T(1024)}, u32[]{:S(2)}) copy-start(f32[2048]{0:T(1024)} %copy-done.18) | copy-start | bytes 24580
  555.3 201.7 %reduce-scatter.35.cloned.1.call-start = ((), (), s32[]{:S(2)}) async-start(), calls=%async_computation.23 | async-start | bytes 1081344
  560.5 8.4 copy-start.12
  565.8 328.1 %reduce-scatter.23.cloned.1.call-start = ((), (), s32[]{:S(2)}) async-start(), calls=%async_computation.17 | async-start | bytes 2162688 | tf_op jit(solution)/shard_map/reduce_scatter | solution.py:213
  568.8 414.5 %reduce-scatter.25.cloned.1.call-start = ((), (), s32[]{:S(2)}) async-start(), calls=%async_computation.18 | async-start | bytes 4718592 | tf_op jit(solution)/shard_map/reduce_scatter | solution.py:206
  576.2 499.1 %reduce-scatter.21.cloned.1.call-start = ((), (), s32[]{:S(2)}) async-start(), calls=%async_computation.16 | async-start | bytes 4718592 | tf_op jit(solution)/shard_map/reduce_scatter | solution.py:204
  582.0 776.9 %reduce-scatter.29.cloned.1.call-start = ((), (), s32[]{:S(2)}) async-start(), calls=%async_computation.20 | async-start | bytes 18874368 | tf_op jit(solution)/shard_map/reduce_scatter | solution.py:209
  596.2 1045.5 %reduce-scatter.27.cloned.1.call-start = ((), (), s32[]{:S(2)}) async-start(), calls=%async_computation.19 | async-start | bytes 18874368 | tf_op jit(solution)/shard_map/reduce_scatter | solution.py:207
  (17 other events, 65.2 us)
Sparse Core Ops, SparseCore 0:
  20.6 39.7 all-gather.2
  61.9 27.3 all-gather.4
  91.7 119.5 all-reduce.6
  257.0 119.7 all-reduce.8
  379.2 37.9 reduce-scatter.16
  427.1 42.3 reduce-scatter.18
  472.9 66.0 reduce-scatter.32
  555.4 63.4 reduce-scatter.30
  621.2 135.7 reduce-scatter.34
  759.7 134.2 reduce-scatter.22
  898.2 85.1 reduce-scatter.24
  987.4 87.9 reduce-scatter.20
  1079.7 279.1 reduce-scatter.28
  1363.1 278.6 reduce-scatter.26
where the time goes:
time: 1650 us
  waiting for transfers between devices  1240 us (75%)
  matrix products  150 us (9%)
  blocking collectives  139 us (8%)
  other arithmetic  64.6 us (4%)
  local copies, waits for them, and re-layouts  38.7 us (2%)
    reduce_scatter x1, waiting for transfers between devices, shards(): lax.psum_scatter(g_w_down, ('dp', 'seq'), scatter_dimension=1, tiled=True)  284 us
    reduce_scatter x1, waiting for transfers between devices, shards(): lax.psum_scatter(g_w_up, ('dp', 'seq'), scatter_dimension=0, tiled=True)  283 us
    unnamed x2, blocking collectives  139 us
    reduce_scatter x1, waiting for transfers between devices, shards(): lax.psum_scatter(g_w_kv, ('dp', 'seq', 'tensor'), scatter_dimension=0, ti...  136 us
    psum x1, waiting for transfers between devices, shards(): residual = x_float + (lax.psum(attn_part, 'tensor') + b_out)  118 us
    psum x1, waiting for transfers between devices, shards(): grad_n2 = lax.psum(grad_a2, 'tensor')  107 us
    unnamed x17, waiting for transfers between devices  100 us
    reduce_scatter x1, waiting for transfers between devices, shards(): lax.psum_scatter(g_w_query, ('dp', 'seq'), scatter_dimension=0, tiled=True)  92 us
  transfers between devices with their start and end apart: 14, of which 10 were waited for; matrix products, arithmetic and copies ran while one was open for 11% of the time, Pallas kernels for 0%

commit v1 on v0

--- a/solution.py
+++ b/solution.py
@@ -142,7 +142,9 @@
     g_w_up = across_rows(flat_two, grad_pre)
     g_b_up = jnp.sum(grad_pre.astype(jnp.float32), axis=0)
     grad_a2 = times_transposed(grad_pre, w_up).reshape(n_rows, seq_len, model_width)
-    grad_n2 = lax.psum(grad_a2, "tensor")
+    grad_n2 = grad_a2
+    for hop in (1, 2):
+        grad_n2 = grad_n2 + lax.ppermute(grad_n2, "tensor", [(dev, dev ^ hop) for dev in range(4)])
     grad_resid = grad_y + norm_back(grad_n2, normed_x2, inv_two, ln2_gain)
     grad_resid_low = grad_resid.astype(jnp.bfloat16)
     grad_resid_own = own_rows(grad_resid)

time: 1650 us -> 1710 us (1.036)
  waiting for transfers between devices: 1240 us -> 1290 us
    ppermute x0 -> x2, waiting for transfers between devices: none -> 151 us  [shards(): lax.ppermute(grad_n2, 'tensor', [(dev, dev ^ hop) for dev in range(4)])]
    psum x1 -> x0, waiting for transfers between devices: 107 us -> none  [shards(): grad_n2 = lax.psum(grad_a2, 'tensor')]
    unnamed x17 -> x16, waiting for transfers between devices: 100 us -> 104 us
  transfers between devices with their start and end apart: 14 -> 15, of which waited for: 10 -> 11; matrix products, arithmetic and copies ran while one was open for 11% -> 11% of each run, Pallas kernels for 0% -> 0%
where the time goes in v1:
time: 1710 us; the launch traced here: 1700 us
  waiting for transfers between devices  1290 us (75%)
  matrix products  148 us (9%)
  blocking collectives  137 us (8%)
  other arithmetic  75.6 us (4%)
  local copies, waits for them, and re-layouts  37.7 us (2%)
    reduce_scatter x1, waiting for transfers between devices, shards(): lax.psum_scatter(g_w_down, ('dp', 'seq'), scatter_dimension=1, tiled=True)  283 us
    reduce_scatter x1, waiting for transfers between devices, shards(): lax.psum_scatter(g_w_up, ('dp', 'seq'), scatter_dimension=0, tiled=True)  283 us
    ppermute x2, waiting for transfers between devices, shards(): lax.ppermute(grad_n2, 'tensor', [(dev, dev ^ hop) for dev in range(4)])  151 us
    unnamed x2, blocking collectives  137 us
    reduce_scatter x1, waiting for transfers between devices, shards(): lax.psum_scatter(g_w_kv, ('dp', 'seq', 'tensor'), scatter_dimension=0, ti...  136 us
    psum x1, waiting for transfers between devices, shards(): residual = x_float + (lax.psum(attn_part, 'tensor') + b_out)  118 us
    unnamed x16, waiting for transfers between devices  104 us
    reduce_scatter x1, waiting for transfers between devices, shards(): lax.psum_scatter(g_w_query, ('dp', 'seq'), scatter_dimension=0, tiled=True)  92.2 us
  transfers between devices with their start and end apart: 15, of which 11 were waited for; matrix products, arithmetic and copies ran while one was open for 11% of the time, Pallas kernels for 0%

profile of v1, /device:TPU:0, one launch (start us, length us, event | category | flops | bytes accessed | tf_op | source)
XLA Modules:
  0.0 1703.6 jit_solution(18213577887150798395)
XLA Ops:
  21.6 5.2 multiply_convert_fusion.3
  30.6 29.8 %all-gather.3.cloned.1.call-done = bf16[3,1024,256]{2,1,0:T(8,128)(2,1)} async-done(((bf16[3,256,256]{2,1,0:T(8,128)(2,1)}), bf16[3,1024,256]{2,1,0:T(8,128)(2,1)}) %all-gather.3.cloned.1.call-update) | async-done | bytes 1572880 | tf_op jit(solution)/shard_map/all_gather | solution.py:88
  60.4 7.9 fusion.4
  68.3 7.4 fusion.3
  75.8 6.5 fusion.28
  93.4 117.9 %all-reduce.6.cloned.1.call-done = f32[3,256,2048]{2,1,0:T(8,128)} async-done(((f32[3,256,2048]{2,1,0:T(8,128)}), f32[3,256,2048]{2,1,0:T(8,128)}) %all-reduce.6.cloned.1.call-update) | async-done | bytes 6291472 | tf_op jit(solution)/shard_map/psum | solution.py:114
  211.3 4.6 fusion.48
  224.9 6.7 fusion.49
  231.7 16.3 convert_reduce_fusion.1
  248.0 8.6 fusion.50
  256.7 10.1 collective-permute-done
  271.3 13.1 convolution_convert_fusion
  284.5 141.0 %collective-permute-done.1 = f32[3,256,2048]{2,1,0:T(8,128)} collective-permute-done((f32[3,256,2048]{2,1,0:T(8,128)}, f32[3,256,2048]{2,1,0:T(8,128)}, u32[]{:S(2)}, u32[]{:S(2)}) %collective-permute-start.1) | collective-permute-done | bytes 6291488 | tf_op jit(solution)/shard_map/ppermute | solution.py:147
  425.5 9.9 multiply_reduce_fusion.2
  435.4 9.0 fusion.47
  453.6 8.6 fusion
  462.2 6.6 fusion.2
  475.7 5.4 multiply_convert_fusion
  489.5 9.7 fusion.25
  507.2 5.0 copy.69
  512.2 95.3 %all-reduce.7 = bf16[3,1024,256]{2,0,1:T(4,128)(2,1)} all-reduce(f32[3,1024,256]{2,0,1:T(4,128)} %copy.69), channel_id=4, replica_groups=mesh['dp'=2,'seq'=4,'tensor'=4] {'seq','tensor'}, use_global_device_ids=true, to_apply=%region_12.13.clone | all-reduce | flops 786432 | bytes 4718592
  619.6 6.0 fusion.32
  625.6 5.7 convolution_multiply_fusion
  631.6 14.0 fusion.45
  645.7 12.8 fusion.51
  660.7 41.7 %all-reduce.2 = f32[128]{0:T(128)S(1)} all-reduce(f32[128]{0:T(128)S(1)} %convert_reduce_fusion.4), channel_id=8, replica_groups=mesh['dp'=2,'seq'=4,'tensor'=4] {'dp','seq','tensor'}, use_global_device_ids=true, to_apply=%region_20.21.clone | all-reduce | flops 128 | bytes 1024
  708.3 103.4 %reduce-scatter.35.cloned.1.call-done = f32[64,6]{1,0:T(8,128)} async-done(((f32[2048,6]{1,0:T(8,128)}), f32[64,6]{1,0:T(8,128)}) %reduce-scatter.35.cloned.1.call-update) | async-done | bytes 1552
  813.2 136.2 %reduce-scatter.23.cloned.1.call-done = f32[64,256]{1,0:T(8,128)} async-done(((f32[2048,256]{1,0:T(8,128)}), f32[64,256]{1,0:T(8,128)}) %reduce-scatter.23.cloned.1.call-update) | async-done | bytes 65552 | tf_op jit(solution)/shard_map/reduce_scatter | solution.py:215
  949.4 89.0 %reduce-scatter.25.cloned.1.call-done = f32[512,256]{1,0:T(8,128)} async-done(((f32[512,2048]{1,0:T(8,128)}), f32[512,256]{1,0:T(8,128)}) %reduce-scatter.25.cloned.1.call-update) | async-done | bytes 524304 | tf_op jit(solution)/shard_map/reduce_scatter | solution.py:208
  1038.3 92.2 %reduce-scatter.21.cloned.1.call-done = f32[256,512]{1,0:T(8,128)} async-done(((f32[2048,512]{1,0:T(8,128)}), f32[256,512]{1,0:T(8,128)}) %reduce-scatter.21.cloned.1.call-update) | async-done | bytes 524304 | tf_op jit(solution)/shard_map/reduce_scatter | solution.py:206
  1130.5 283.4 %reduce-scatter.29.cloned.1.call-done = f32[2048,256]{1,0:T(8,128)} async-done(((f32[2048,2048]{1,0:T(8,128)}), f32[2048,256]{1,0:T(8,128)}) %reduce-scatter.29.cloned.1.call-update) | async-done | bytes 2097168 | tf_op jit(solution)/shard_map/reduce_scatter | solution.py:211
  1413.8 283.1 %reduce-scatter.27.cloned.1.call-done = f32[256,2048]{1,0:T(8,128)} async-done(((f32[2048,2048]{1,0:T(8,128)}), f32[256,2048]{1,0:T(8,128)}) %reduce-scatter.27.cloned.1.call-update) | async-done | bytes 2097168 | tf_op jit(solution)/shard_map/reduce_scatter | solution.py:209
  (167 shorter events, 96.1 us)
Async XLA Ops:
  7.2 76.0 %copy-start = (bf16[512,2048]{1,0:T(8,128)(2,1)S(1)}, bf16[512,2048]{1,0:T(8,128)(2,1)}, u32[]{:S(2)}) copy-start(bf16[512,2048]{1,0:T(8,128)(2,1)} %param.26) | copy-start | bytes 6291460
  7.2 6.4 copy-start.20
  7.2 6.4 copy-start.21
  7.2 53.2 %all-gather.3.cloned.1.call-start = ((), (), s32[]{:S(2)}) async-start(), calls=%async_computation.10 | async-start | bytes 1966080 | tf_op jit(solution)/shard_map/all_gather | solution.py:88
  7.3 6.4 copy-start.3
  20.5 68.9 %all-gather.5.cloned.1.call-start = ((), (), s32[]{:S(2)}) async-start(), calls=%async_computation.13 | async-start | bytes 3932160 | tf_op jit(solution)/shard_map/all_gather | solution.py:135
  21.2 190.1 %all-reduce.6.cloned.1.call-start = ((), (), s32[]{:S(2)}) async-start(), calls=%async_computation.11 | async-start | bytes 12582912 | tf_op jit(solution)/shard_map/psum | solution.py:114
  21.6 8.2 copy-start.27
  68.3 7.5 copy-start.7
  87.7 396.1 %reduce-scatter.17.cloned.1.call-start = ((), (), s32[]{:S(2)}) async-start(), calls=%async_computation.12 | async-start | bytes 3932160 | tf_op jit(solution)/shard_map/reduce_scatter | solution.py:129
  215.9 6.2 copy-start.1
  216.7 8.2 slice-start.3
  222.1 9.5 copy-start.13
  224.9 6.8 copy-start.12
  231.7 16.4 copy-start.30
  256.6 10.2 collective-permute-start
  270.8 154.7 %collective-permute-start.1 = (f32[3,256,2048]{2,1,0:T(8,128)}, f32[3,256,2048]{2,1,0:T(8,128)}, u32[]{:S(2)}, u32[]{:S(2)}) collective-permute-start(f32[3,256,2048]{2,1,0:T(8,128)} %add.189), channel_id=1, source_target_pairs={{0,2},{1,3},{2,0},{3,1},{4,6},{5,7},{6,4},{7,5},{8,10},{9,11},{10,... | collective-permute-start | bytes 18874376 | tf_op jit(solution)/shard_map/ppermute | solution.py:147
  284.4 325.4 %reduce-scatter.19.cloned.1.call-start = ((), (), s32[]{:S(2)}) async-start(), calls=%async_computation.14 | async-start | bytes 3932160 | tf_op jit(solution)/shard_map/reduce_scatter | solution.py:189
  462.2 9.4 copy-start.8
  481.1 178.2 %reduce-scatter.33.cloned.1.call-start = ((), (), s32[]{:S(2)}) async-start(), calls=%async_computation.21 | async-start | bytes 73728
  483.3 219.8 %reduce-scatter.31.cloned.1.call-start = ((), (), s32[]{:S(2)}) async-start(), calls=%async_computation.20 | async-start | bytes 73728
  487.1 12.2 slice-start
  489.5 9.7 slice-start.1
  489.5 9.7 copy-start.5
  507.2 102.6 %copy-start.17 = (f32[2048]{0:T(1024)S(1)}, f32[2048]{0:T(1024)}, u32[]{:S(2)}) copy-start(f32[2048]{0:T(1024)} %copy-done.16) | copy-start | bytes 24580
  609.7 8.5 copy-start.11
  609.7 202.0 %reduce-scatter.35.cloned.1.call-start = ((), (), s32[]{:S(2)}) async-start(), calls=%async_computation.22 | async-start | bytes 1081344
  615.1 334.2 %reduce-scatter.23.cloned.1.call-start = ((), (), s32[]{:S(2)}) async-start(), calls=%async_computation.16 | async-start | bytes 2162688 | tf_op jit(solution)/shard_map/reduce_scatter | solution.py:215
  618.2 420.2 %reduce-scatter.25.cloned.1.call-start = ((), (), s32[]{:S(2)}) async-start(), calls=%async_computation.17 | async-start | bytes 4718592 | tf_op jit(solution)/shard_map/reduce_scatter | solution.py:208
  625.6 504.9 %reduce-scatter.21.cloned.1.call-start = ((), (), s32[]{:S(2)}) async-start(), calls=%async_computation.15 | async-start | bytes 4718592 | tf_op jit(solution)/shard_map/reduce_scatter | solution.py:206
  631.4 782.4 %reduce-scatter.29.cloned.1.call-start = ((), (), s32[]{:S(2)}) async-start(), calls=%async_computation.19 | async-start | bytes 18874368 | tf_op jit(solution)/shard_map/reduce_scatter | solution.py:211
  645.7 1051.2 %reduce-scatter.27.cloned.1.call-start = ((), (), s32[]{:S(2)}) async-start(), calls=%async_computation.18 | async-start | bytes 18874368 | tf_op jit(solution)/shard_map/reduce_scatter | solution.py:209
  (18 other events, 73.7 us)
Sparse Core Ops, SparseCore 0:
  20.6 39.7 all-gather.2
  61.9 27.3 all-gather.4
  91.7 119.5 all-reduce.5
  284.5 55.6 reduce-scatter.16
  481.2 37.9 reduce-scatter.18
  522.5 62.5 reduce-scatter.32
  609.8 63.9 reduce-scatter.30
  676.1 135.6 reduce-scatter.34
  814.6 134.7 reduce-scatter.22
  953.4 84.8 reduce-scatter.24
  1042.5 87.9 reduce-scatter.20
  1134.7 279.1 reduce-scatter.28
  1418.2 278.6 reduce-scatter.26
